TPU v7x, 32 devices: a whole 2x2x4 slice. The times are simulated.
32 devices in a mesh: tm: 8 (over z, x), frame: 4 (over y, core).
Axes of the slice: x: 2, y: 2, z: 4, core: 2. Of those that a mesh axis runs over, the one named last changes fastest.
Arguments:
- start_state: float32 [4, 32, 32, 128], P('frame'), may hold values from -6 to 6
- initial_guess: float32 [8, 4, 32, 32, 128], P('tm', 'frame'), may hold values from -6 to 6
- noise_draws: float32 [8, 4, 32, 32, 128], P('tm', 'frame'), may hold values from -6 to 6
- timesteps: int32 [8], P('tm'), may hold values from 0 to 999
- gain_space: float32 [128], replicated, may hold values from 0.1 to 1.9
- gain_attention: float32 [128], replicated, may hold values from 0.1 to 1.9
- time_weight: float32 [128, 256], replicated, may hold values from -0.5 to 0.5
- space_weight: bfloat16 [1152, 128], replicated, may hold values from -0.1875 to 0.1875
- attention_weight: bfloat16 [128, 384], replicated, may hold values from -4 to 4
- output_weight: bfloat16 [128, 128], replicated, may hold values from -0.5 to 0.5
Outputs:
- advanced: float32 [8, 4, 32, 32, 128], P('tm', 'frame')
All inputs are finite; a program needn't handle non-finite values.
Results may differ from a plain program's by a relative error of at most 0.0025.
Values may be sent and summed in bfloat16 or wider, within the bound.
A program may use at most 64 MiB of HBM per device.

v0:
```python
import math

import jax
import jax.numpy as jnp
from jax import lax
from jax.sharding import PartitionSpec as P

C = 128
HEAD_DIM = 64
ITERS = 2


def carried_in(part, axis, combine, identity):
    place = lax.axis_index(axis)
    gathered = lax.all_gather(part, axis)
    state = jnp.zeros_like(part) + jnp.asarray(identity, part.dtype)

    def one(hop, state):
        return combine(state, lax.dynamic_index_in_dim(gathered, hop, 0, False))

    return lax.fori_loop(0, place, one, state)


def embed_time(step_value):
    half_width = C // 2
    frequency = jnp.exp(-math.log(10000.0) * jnp.arange(half_width, dtype=jnp.float32) / half_width)
    angles = step_value.astype(jnp.float32) * frequency
    return jnp.concatenate([jnp.cos(angles), jnp.sin(angles)])


def modulation(step_value, time_weight):
    encoded = embed_time(step_value)[None, :]
    shifted = jnp.dot(
        encoded, time_weight, precision=lax.Precision.HIGHEST, preferred_element_type=jnp.float32
    )[0]
    return (1.0 + shifted[:C], shifted[C:])


def normalize(field, gain):
    return field * lax.rsqrt(jnp.mean(field * field, axis=-1, keepdims=True) + 1e-06) * gain


def conv_taps(padded, space_weight):
    frames_here = padded.shape[0]
    rows_here = padded.shape[1] - 2
    cols_here = padded.shape[2] - 2
    shifted = [
        padded[:, row_shift : row_shift + rows_here, col_shift : col_shift + cols_here, :]
        for row_shift in range(3)
        for col_shift in range(3)
    ]
    stacked = jnp.concatenate(shifted, axis=-1).reshape(-1, 9 * padded.shape[3])
    result = jnp.dot(stacked, space_weight, preferred_element_type=jnp.float32)
    return result.reshape(frames_here, rows_here, cols_here, space_weight.shape[1])


def attend(normed_in, attention_weight):
    frames_all, rows_here, cols_here, channels = normed_in.shape
    head_count = channels // HEAD_DIM
    projected = jnp.dot(
        normed_in.reshape(-1, channels), attention_weight, preferred_element_type=jnp.float32
    ).astype(jnp.bfloat16)
    projected = projected.reshape(frames_all, rows_here, cols_here, 3, head_count, HEAD_DIM)
    scores = jnp.einsum(
        "fxyhd,gxyhd->xyhfg",
        projected[:, :, :, 0],
        projected[:, :, :, 1],
        preferred_element_type=jnp.float32,
    ) / math.sqrt(HEAD_DIM)
    weights = jax.nn.softmax(scores, axis=-1).astype(jnp.bfloat16)
    attended = jnp.einsum(
        "xyhfg,gxyhd->fxyhd", weights, projected[:, :, :, 2], preferred_element_type=jnp.float32
    )
    return attended.reshape(frames_all, rows_here, cols_here, channels).astype(jnp.bfloat16)


def add_terms(earlier, later):
    return earlier + later


def prefix_before(term):
    return carried_in(term, "tm", add_terms, jnp.zeros_like(term))


def shards(
    start_state,
    initial_guess,
    noise_draws,
    timesteps,
    gain_space,
    gain_attention,
    time_weight,
    space_weight,
    attention_weight,
    output_weight,
):
    step_value = timesteps[0]
    time_value = step_value.astype(jnp.float32) / 1000.0
    coefficient = (0.5 + time_value) / math.sqrt(lax.axis_size("tm"))
    scaling, offset = modulation(step_value, time_weight)
    guess_here = initial_guess[0]
    noise_here = noise_draws[0]
    state = guess_here
    term = jnp.zeros_like(guess_here)
    before = jnp.zeros_like(guess_here)
    for picard_turn in range(ITERS):
        evaluate_normed = (normalize(state, gain_space) * scaling + offset).astype(jnp.bfloat16)
        mixed_state = state + jax.nn.silu(
            conv_taps(jnp.pad(evaluate_normed, ((0, 0), (1, 1), (1, 1), (0, 0))), space_weight)
        )
        attended = attend(
            lax.all_to_all(
                normalize(mixed_state, gain_attention).astype(jnp.bfloat16),
                "frame",
                split_axis=1,
                concat_axis=0,
                tiled=True,
            ),
            attention_weight,
        )
        evaluate_attended = lax.all_to_all(
            attended, "frame", split_axis=0, concat_axis=1, tiled=True
        )
        projected = jnp.dot(
            evaluate_attended.reshape(-1, evaluate_attended.shape[-1]),
            output_weight,
            preferred_element_type=jnp.float32,
        )
        evaluated = mixed_state + projected.reshape(mixed_state.shape)
        term = coefficient * (evaluated + time_value * noise_here)
        before = prefix_before(term)
        state = start_state + before
    advanced = start_state + (before + term)
    return advanced[None]


def solution(mesh):
    return jax.shard_map(
        shards,
        mesh=mesh,
        in_specs=(
            P("frame", None, None, None),
            P("tm", "frame", None, None, None),
            P("tm", "frame", None, None, None),
            P("tm"),
            P(),
            P(),
            P(),
            P(),
            P(),
            P(),
        ),
        out_specs=P("tm", "frame", None, None, None),
        check_vma=False,
    )
```

profile of v0, /device:TPU:24, one launch (start us, length us, event | category | flops | bytes accessed | tf_op | source)
XLA Modules:
  0.0 241.2 jit_solution(15399592069177825315)
XLA Ops:
  7.3 1.1 fusion.36
  8.4 1.2 fusion.17
  9.8 1.2 fusion.21
  11.1 0.3 pad_slice_fusion.8
  11.7 0.4 copy-done.1
  12.1 0.3 constant_dynamic-update-slice_fusion.4
  12.7 0.8 fusion.46
  13.5 0.2 multiply_reduce_fusion.2
  13.9 8.6 %all_to_all.16 = bf16[1,32,32,128]{3,2,0,1:T(8,128)(2,1)S(1)} all-to-all(bf16[1,32,32,128]{3,2,0,1:T(8,128)(2,1)S(1)} %fusion.32), channel_id=1, replica_groups=mesh['tm'=8,'frame'=4] {'frame'}, dimensions={1} | all-to-all | bytes 524288 | tf_op jit(solution)/shard_map/all_to_all | solution.py:112
  22.5 1.2 convolution_convert_fusion.1
  23.8 3.3 %reshape.327 = bf16[4,8,32,3,2,64]{5,4,3,2,1,0:T(2,128)(2,1)S(1)} reshape(bf16[1024,384]{1,0:T(8,128)(2,1)} %convolution_convert_fusion.1) | data formatting | bytes 1572864 | tf_op jit(solution)/shard_map/reshape | solution.py:63
  27.1 2.7 %fusion.43 = (bf16[4,8,32,1,2,64]{5,4,3,2,1,0:T(2,128)(2,1)S(1)}, bf16[4,8,32,1,2,64]{5,4,3,2,1,0:T(2,128)(2,1)}, bf16[4,8,32,1,2,64]{5,4,3,2,1,0:T(2,128)(2,1)}) fusion(bf16[4,8,32,3,2,64]{5,4,3,2,1,0:T(2,128)(2,1)S(1)} %reshape.327), kind=kLoop, calls=%fused_computation.107 | loop fusion | bytes 1572864 | tf_op jit(solution)/shard_map/slice | solution.py:72
  29.8 3.2 %fusion.44 = (f32[8,32,2,4]{3,2,1,0:T(2,128)S(1)}, f32[8,32,2,4,4]{3,4,2,1,0:T(4,128)S(1)}) fusion(bf16[4,8,32,1,2,64]{5,4,3,2,1,0:T(2,128)(2,1)} %get-tuple-element.102, bf16[4,8,32,1,2,64]{5,4,3,2,1,0:T(2,128)(2,1)} %get-tuple-element.101), kind=kOutput, calls=%fused_computation.108 | convolution fusion | flops 1073155 | bytes 565248 | tf_op jit(solution)/shard_map/sub | solution.py:70
  33.0 0.9 fusion.6
  33.9 0.5 copy.38
  34.4 1.0 convert_element_type.80
  35.4 3.4 %all-to-all-start.1 = ((bf16[4,8,32,128]{3,2,1,0:T(8,128)(2,1)}), bf16[4,8,32,128]{3,2,1,0:T(8,128)(2,1)S(1)}, u32[]{:S(2)}, u32[]{:S(2)}) async-start(bf16[4,8,32,128]{3,2,1,0:T(8,128)(2,1)} %convert_element_type.80), calls=%async_computation.1 | async-start | bytes 524288 | tf_op jit(solution)/shard_map/all_to_all | solution.py:121
  38.9 5.9 %all-to-all-done.1 = bf16[4,8,32,128]{3,2,1,0:T(8,128)(2,1)S(1)} async-done(((bf16[4,8,32,128]{3,2,1,0:T(8,128)(2,1)}), bf16[4,8,32,128]{3,2,1,0:T(8,128)(2,1)S(1)}, u32[]{:S(2)}, u32[]{:S(2)}) %all-to-all-start.1) | async-done | bytes 262176 | tf_op jit(solution)/shard_map/all_to_all | solution.py:121
  44.8 1.1 fusion.9
  45.9 71.4 %all-gather.5.cloned.1.call-done = f32[256,32,128]{2,1,0:T(8,128)} async-done(((f32[32,32,128]{2,1,0:T(8,128)}), f32[256,32,128]{2,1,0:T(8,128)}) %all-gather.5.cloned.1.call-update) | async-done | bytes 4194320 | tf_op jit(solution)/shard_map/all_gather | solution.py:15
  117.4 7.5 %while.20 = (s32[]{:T(128)}, f32[1,32,32,128]{3,2,1,0:T(8,128)S(1)}, s32[]{:T(128)}, f32[8,1,32,32,128]{4,3,2,1,0:T(8,128)}, s32[]{:T(128)}, /*index=5*/s32[]{:T(128)}, s32[]{:T(128)}) while((s32[]{:T(128)}, f32[1,32,32,128]{3,2,1,0:T(8,128)S(1)}, s32[]{:T(128)}, f32[8,1,32,32,128]{4,3,2,1,0:T(8,128)}, s32[]{:T(128)}, /*index=5*/s32[]{:T(128)}, ...), condition=%wide.region_5.6_spmd, body=%wide.region_4.5_spmd.sunk | while | flops 131077 | bytes 1572979 | solution.py:21
  117.5 1.2 bitcast_add_fusion.6
  118.7 1.2 bitcast_add_fusion.6
  119.9 1.2 bitcast_add_fusion.6
  121.2 1.2 bitcast_add_fusion.6
  122.4 1.2 bitcast_add_fusion.6
  123.6 1.2 bitcast_add_fusion.6
  125.8 0.3 constant_dynamic-update-slice_fusion.9
  126.5 0.8 fusion.47
  127.7 8.5 %all_to_all.17 = bf16[1,32,32,128]{3,2,0,1:T(8,128)(2,1)S(1)} all-to-all(bf16[1,32,32,128]{3,2,0,1:T(8,128)(2,1)S(1)} %fusion.33), channel_id=1, replica_groups=mesh['tm'=8,'frame'=4] {'frame'}, dimensions={1} | all-to-all | bytes 524288 | tf_op jit(solution)/shard_map/all_to_all | solution.py:112
  136.3 0.3 convolution_convert_fusion
  136.6 0.8 reshape.331
  137.5 2.5 %fusion.42 = (bf16[4,8,32,1,2,64]{5,4,3,2,1,0:T(2,128)(2,1)S(1)}, bf16[4,8,32,1,2,64]{5,4,3,2,1,0:T(2,128)(2,1)S(1)}, bf16[4,8,32,1,2,64]{5,4,3,2,1,0:T(2,128)(2,1)}) fusion(bf16[4,8,32,3,2,64]{5,4,3,2,1,0:T(2,128)(2,1)S(1)} %reshape.331), kind=kLoop, calls=%fused_computation.106 | loop fusion | bytes 1572864 | tf_op jit(solution)/shard_map/slice | solution.py:72
  140.0 3.1 %fusion.45 = (f32[8,32,2,4]{3,2,1,0:T(2,128)S(1)}, f32[8,32,2,4,4]{3,4,2,1,0:T(4,128)S(1)}) fusion(bf16[4,8,32,1,2,64]{5,4,3,2,1,0:T(2,128)(2,1)} %get-tuple-element.99, bf16[4,8,32,1,2,64]{5,4,3,2,1,0:T(2,128)(2,1)S(1)} %get-tuple-element.98), kind=kOutput, calls=%fused_computation.109 | convolution fusion | flops 1073155 | bytes 565248 | tf_op jit(solution)/shard_map/sub | solution.py:70
  143.1 0.9 fusion.7
  143.9 0.5 copy.45
  144.5 0.2 convert_element_type.87
  144.8 8.4 %all_to_all.18 = bf16[4,8,32,128]{3,2,1,0:T(8,128)(2,1)S(1)} all-to-all(bf16[4,8,32,128]{3,2,1,0:T(8,128)(2,1)S(1)} %convert_element_type.87), channel_id=1, replica_groups=mesh['tm'=8,'frame'=4] {'frame'}, dimensions={0} | all-to-all | bytes 524288 | tf_op jit(solution)/shard_map/all_to_all | solution.py:121
  153.2 1.0 fusion.12
  154.2 71.8 %all-gather.7.cloned.1.call-done = f32[8,32,32,128]{3,2,1,0:T(8,128)} async-done(((f32[1,32,32,128]{3,2,1,0:T(8,128)}), f32[8,32,32,128]{3,2,1,0:T(8,128)}) %all-gather.7.cloned.1.call-update) | async-done | bytes 4194320 | tf_op jit(solution)/shard_map/all_gather | solution.py:15
  226.0 7.4 %while.21 = (s32[]{:T(128)}, f32[1,32,32,128]{3,2,1,0:T(8,128)S(1)}, s32[]{:T(128)}, f32[8,1,32,32,128]{4,3,2,1,0:T(8,128)}, s32[]{:T(128)}, /*index=5*/s32[]{:T(128)}, s32[]{:T(128)}) while((s32[]{:T(128)}, f32[1,32,32,128]{3,2,1,0:T(8,128)S(1)}, s32[]{:T(128)}, f32[8,1,32,32,128]{4,3,2,1,0:T(8,128)}, s32[]{:T(128)}, ...), condition=%wide.region_11.12_spmd, body=%wide.region_10.11_spmd.sunk | while | flops 131077 | bytes 1572979 | solution.py:21
  226.1 1.3 bitcast_add_fusion.7
  227.4 1.2 bitcast_add_fusion.7
  228.6 1.2 bitcast_add_fusion.7
  229.8 1.2 bitcast_add_fusion.7
  231.0 1.2 bitcast_add_fusion.7
  232.2 1.2 bitcast_add_fusion.7
  233.4 0.9 add_bitcast_fusion
  (57 shorter events, 2.8 us)
Async XLA Ops:
  6.5 6.1 %copy-start = (bf16[1152,128]{1,0:T(8,128)(2,1)S(1)}, bf16[1152,128]{1,0:T(8,128)(2,1)}, u32[]{:S(2)}) copy-start(bf16[1152,128]{1,0:T(8,128)(2,1)} %param.21) | copy-start | bytes 884740
  11.0 1.0 copy-start.1
  11.0 1.0 copy-start.10
  12.6 1.1 copy-start.11
  13.4 9.1 %copy-start.7 = (bf16[128,384]{1,0:T(8,128)(2,1)S(1)}, bf16[128,384]{1,0:T(8,128)(2,1)}, u32[]{:S(2)}) copy-start(bf16[128,384]{1,0:T(8,128)(2,1)} %param.22) | copy-start | bytes 294916
  33.9 10.9 %copy-start.5 = (f32[1,1,32,32,128]{4,3,2,1,0:T(8,128)S(1)}, f32[1,1,32,32,128]{4,3,2,1,0:T(8,128)}, u32[]{:S(2)}) copy-start(f32[1,1,32,32,128]{4,3,2,1,0:T(8,128)} %param.16) | copy-start | bytes 1572868
  33.9 10.9 %copy-start.8 = (bf16[128,128]{1,0:T(8,128)(2,1)S(1)}, bf16[128,128]{1,0:T(8,128)(2,1)}, u32[]{:S(2)}) copy-start(bf16[128,128]{1,0:T(8,128)(2,1)} %param.23) | copy-start | bytes 98308
  35.4 9.4 %all-to-all-start.1 = ((bf16[4,8,32,128]{3,2,1,0:T(8,128)(2,1)}), bf16[4,8,32,128]{3,2,1,0:T(8,128)(2,1)S(1)}, u32[]{:S(2)}, u32[]{:S(2)}) async-start(bf16[4,8,32,128]{3,2,1,0:T(8,128)(2,1)} %convert_element_type.80), calls=%async_computation.1 | async-start | bytes 524288 | tf_op jit(solution)/shard_map/all_to_all | solution.py:121
  38.8 78.6 %all-gather.5.cloned.1.call-start = ((), (), s32[]{:S(2)}) async-start(), calls=%async_computation.4 | async-start | bytes 4718592 | tf_op jit(solution)/shard_map/all_gather | solution.py:15
  45.9 180.1 %all-gather.7.cloned.1.call-start = ((), (), s32[]{:S(2)}) async-start(), calls=%async_computation.5 | async-start | bytes 4718592 | tf_op jit(solution)/shard_map/all_gather | solution.py:15
  117.4 7.5 %copy-start.3 = (f32[1,32,32,128]{3,2,1,0:T(8,128)S(1)}, f32[1,32,32,128]{3,2,1,0:T(8,128)}, u32[]{:S(2)}) copy-start(f32[1,32,32,128]{3,2,1,0:T(8,128)} %param.14) | copy-start | bytes 1572868
  143.9 9.2 %copy-start.6 = (f32[1,1,32,32,128]{4,3,2,1,0:T(8,128)S(1)}, f32[1,1,32,32,128]{4,3,2,1,0:T(8,128)}, u32[]{:S(2)}) copy-start(f32[1,1,32,32,128]{4,3,2,1,0:T(8,128)} %param.16) | copy-start | bytes 1572868
  143.9 9.2 %copy-start.9 = (bf16[128,128]{1,0:T(8,128)(2,1)S(1)}, bf16[128,128]{1,0:T(8,128)(2,1)}, u32[]{:S(2)}) copy-start(bf16[128,128]{1,0:T(8,128)(2,1)} %param.23) | copy-start | bytes 98308
  226.0 7.4 %copy-start.2 = (f32[1,32,32,128]{3,2,1,0:T(8,128)S(1)}, f32[1,32,32,128]{3,2,1,0:T(8,128)}, u32[]{:S(2)}) copy-start(f32[1,32,32,128]{3,2,1,0:T(8,128)} %fusion.12) | copy-start | bytes 1572868
  226.0 7.4 %copy-start.4 = (f32[1,32,32,128]{3,2,1,0:T(8,128)S(1)}, f32[1,32,32,128]{3,2,1,0:T(8,128)}, u32[]{:S(2)}) copy-start(f32[1,32,32,128]{3,2,1,0:T(8,128)} %param.14) | copy-start | bytes 1572868
Sparse Core Ops, SparseCore 0:
  46.0 71.3 all-gather.4
  154.3 71.6 all-gather.6
where the time goes:
time: 243 us; the launch traced here: 241 us
  waiting for transfers between devices  149 us (61%)
  blocking collectives  25.5 us (10%)
  other arithmetic  19.7 us (8%)
  between operations  14.6 us (6%)
  matrix products  14.3 us (6%)
  local copies, waits for them, and re-layouts  13.9 us (6%)
  starting transfers between devices  3.49 us (1%)
    all_gather x2, waiting for transfers between devices, carried_in(): gathered = lax.all_gather(part, axis)  143 us
    all_to_all x2, blocking collectives, shards(): lax.all_to_all(normalize(mixed_state, gain_attention).astype(jnp.bfloat16...  17.1 us
    add x12, other arithmetic, add_terms(): return earlier + later  14.4 us
    all_to_all x1, blocking collectives, shards(): lax.all_to_all(attended, 'frame', split_axis=0, concat_axis=1, tiled=True)  8.39 us
    sub x2, matrix products, attend(): weights = jax.nn.softmax(scores, axis=-1).astype(jnp.bfloat16)  6.26 us
    all_to_all x1, waiting for transfers between devices, shards(): lax.all_to_all(attended, 'frame', split_axis=0, concat_axis=1, tiled=True)  5.91 us
    slice x2, local copies, waits for them, and re-layouts, attend(): projected[:, :, :, 2]  5.22 us
  transfers between devices with their start and end apart: 3, of which 3 were waited for; matrix products, arithmetic and copies ran while one was open for 0% of the time, Pallas kernels for 0%

commit v1 on v0

v1 whole, which is shorter than its diff:
```python
import functools
import math

import jax
import jax.numpy as jnp
from jax import lax
from jax.experimental import pallas as pl
from jax.experimental.pallas import tpu as pltpu
from jax.sharding import PartitionSpec as P

HEAD_DIM = 64
ITERS = 2
PIECES = 4
EPS = 1e-06


def modulation(step_value, time_weight):
    channels = time_weight.shape[0]
    half_width = channels // 2
    frequency = jnp.exp(-math.log(10000.0) * jnp.arange(half_width, dtype=jnp.float32) / half_width)
    angles = step_value.astype(jnp.float32) * frequency
    encoded = jnp.concatenate([jnp.cos(angles), jnp.sin(angles)])[None, :]
    shifted = jnp.dot(
        encoded, time_weight, precision=lax.Precision.HIGHEST, preferred_element_type=jnp.float32
    )[0]
    return (1.0 + shifted[:channels], shifted[channels:])


def kernel(
    n_tm,
    n_frame,
    width,
    start_ref,
    guess_ref,
    noise_ref,
    rows_ref,
    wconv_ref,
    wattn_ref,
    wout_ref,
    out_ref,
    state,
    taps,
    mixed,
    term,
    proj,
    ain,
    rin,
    aout,
    rout,
    zin,
    zout,
    xin,
    in_send,
    in_recv,
    out_send,
    out_recv,
    z_send,
    z_recv,
    x_send,
    x_recv,
):
    cells, channels = start_ref.shape
    share = cells // n_frame
    piece = cells // PIECES
    me_tm = lax.axis_index("tm")
    me = lax.axis_index("frame")
    link = me_tm // 2
    side = lax.rem(me_tm, 2)
    links = n_tm // 2
    has_prev = link > 0
    has_next = link < links - 1

    def at_frame(f):
        return {"tm": me_tm, "frame": f}

    def at_tm(t):
        return {"tm": t, "frame": me}

    def peer(s):
        return lax.rem(me + s, n_frame)

    barrier = pltpu.get_barrier_semaphore()

    def greet(device):
        pl.semaphore_signal(barrier, inc=1, device_id=device, device_id_type=pl.DeviceIdType.MESH)

    for s in range(1, n_frame):
        greet(at_frame(peer(s)))
    greet(at_tm(me_tm + 1 - 2 * side))

    @pl.when(has_prev)
    def _():
        greet(at_tm(me_tm - 2))

    @pl.when(has_next)
    def _():
        greet(at_tm(me_tm + 2))

    def meet():
        pl.semaphore_wait(barrier, n_frame + has_prev.astype(jnp.int32) + has_next.astype(jnp.int32))

    edge = jnp.zeros((width, 3 * channels), jnp.bfloat16)
    taps[0:width, :] = edge
    taps[cells + width : cells + 2 * width, :] = edge

    @pl.when(link == 0)
    def _():
        zin[...] = jnp.zeros_like(zin)

    gain_space = rows_ref[0:1, :]
    offset = rows_ref[1:2, :]
    coefficient = rows_ref[2:3, :]
    time_value = rows_ref[3:4, :]
    gain_attention = rows_ref[4:5, :]

    def inverse_rms(v):
        return lax.rsqrt(jnp.mean(v * v, axis=-1, keepdims=True) + EPS)

    column = lax.broadcasted_iota(jnp.int32, (piece, channels), 0) % width
    head_in = lax.broadcasted_iota(jnp.int32, (2 * channels, channels), 0) % channels // HEAD_DIM
    head_to = lax.broadcasted_iota(jnp.int32, (2 * channels, channels), 1) // HEAD_DIM
    gather_heads = jnp.where(head_in == head_to, 1.0, 0.0).astype(jnp.bfloat16)

    for turn in range(ITERS):
        source = guess_ref if turn == 0 else state

        def make_taps(c, _):
            at = pl.multiple_of(c * piece, piece)
            x = source[pl.ds(at, piece), :]
            normed = x * inverse_rms(x) * gain_space + offset
            left = jnp.where(column == 0, 0.0, pltpu.roll(normed, 1, 0))
            right = jnp.where(column == width - 1, 0.0, pltpu.roll(normed, piece - 1, 0))
            to = pl.multiple_of(at + width, width)
            taps[pl.ds(to, piece), 0:channels] = left.astype(jnp.bfloat16)
            taps[pl.ds(to, piece), channels : 2 * channels] = normed.astype(jnp.bfloat16)
            taps[pl.ds(to, piece), 2 * channels : 3 * channels] = right.astype(jnp.bfloat16)
            return 0

        lax.fori_loop(0, PIECES, make_taps, 0)
        if turn == 0:
            meet()

        def in_copy(s):
            return pltpu.make_async_remote_copy(
                src_ref=ain.at[turn, peer(s)],
                dst_ref=rin.at[turn, me],
                send_sem=in_send.at[turn, s],
                recv_sem=in_recv.at[turn, s],
                device_id=at_frame(peer(s)),
                device_id_type=pl.DeviceIdType.MESH,
            )

        def mix(q):
            at = pl.multiple_of(q * share, share)
            total = jnp.zeros((share, channels), jnp.float32)
            for row in range(3):
                start = pl.multiple_of(at + row * width, width)
                total += jnp.dot(
                    taps[pl.ds(start, share), :],
                    wconv_ref[row * 3 * channels : (row + 1) * 3 * channels, :],
                    preferred_element_type=jnp.float32,
                )
            value = source[pl.ds(at, share), :] + total / (1.0 + jnp.exp(-total))
            mixed[pl.ds(at, share), :] = value
            return (value * inverse_rms(value) * gain_attention).astype(jnp.bfloat16)

        def mix_and_send(s, _):
            q = peer(s)
            ain[turn, q] = mix(q)
            in_copy(s).start()
            return 0

        lax.fori_loop(1, n_frame, mix_and_send, 0)
        rin[turn, me] = mix(me)

        def project(f):
            proj[f] = (
                jnp.dot(rin[turn, f], wattn_ref[...], preferred_element_type=jnp.float32)
                .astype(jnp.bfloat16)
                .astype(jnp.float32)
            )

        project(me)

        def arrive(s, _):
            in_copy(s).wait()
            project(lax.rem(me + n_frame - s, n_frame))
            return 0

        lax.fori_loop(1, n_frame, arrive, 0)

        def attend(f):
            query = proj[f, :, 0:channels]
            products = (query[None] * proj[:, :, channels : 2 * channels]).reshape(-1, channels)
            high = products.astype(jnp.bfloat16)
            low = (products - high.astype(jnp.float32)).astype(jnp.bfloat16)
            scores = jnp.dot(
                jnp.concatenate([high, low], axis=-1), gather_heads, preferred_element_type=jnp.float32
            ).reshape(n_frame, share, channels) * (1.0 / math.sqrt(HEAD_DIM))
            raised = jnp.exp(scores - jnp.max(scores, axis=0, keepdims=True))
            weights = raised / jnp.sum(raised, axis=0, keepdims=True)
            weights = weights.astype(jnp.bfloat16).astype(jnp.float32)
            return jnp.sum(weights * proj[:, :, 2 * channels : 3 * channels], axis=0).astype(jnp.bfloat16)

        def out_copy(s):
            return pltpu.make_async_remote_copy(
                src_ref=aout.at[turn, peer(s)],
                dst_ref=rout.at[turn, me],
                send_sem=out_send.at[turn, s],
                recv_sem=out_recv.at[turn, s],
                device_id=at_frame(peer(s)),
                device_id_type=pl.DeviceIdType.MESH,
            )

        def attend_and_send(s, _):
            f = peer(s)
            aout[turn, f] = attend(f)
            out_copy(s).start()
            return 0

        lax.fori_loop(1, n_frame, attend_and_send, 0)
        rout[turn, me] = attend(me)

        def close(q):
            at = pl.multiple_of(q * share, share)
            drift = mixed[pl.ds(at, share), :] + jnp.dot(
                rout[turn, q], wout_ref[...], preferred_element_type=jnp.float32
            )
            term[pl.ds(at, share), :] = coefficient * (drift + time_value * noise_ref[pl.ds(at, share), :])

        close(me)

        def land(s, _):
            out_copy(s).wait()
            close(lax.rem(me + n_frame - s, n_frame))
            return 0

        lax.fori_loop(1, n_frame, land, 0)

        def z_copy(c):
            return pltpu.make_async_remote_copy(
                src_ref=zout.at[turn, c],
                dst_ref=zin.at[turn, c],
                send_sem=z_send.at[turn, c],
                recv_sem=z_recv.at[turn, c],
                device_id=at_tm(me_tm + 2),
                device_id_type=pl.DeviceIdType.MESH,
            )

        def x_copy(c, src):
            return pltpu.make_async_remote_copy(
                src_ref=src.at[turn, c],
                dst_ref=xin.at[turn, c],
                send_sem=x_send.at[turn, c],
                recv_sem=x_recv.at[turn, c],
                device_id=at_tm(me_tm + 1 - 2 * side),
                device_id_type=pl.DeviceIdType.MESH,
            )

        def chain(c, _):
            at = pl.multiple_of(c * piece, piece)

            @pl.when(has_prev)
            def _():
                z_copy(c).wait_recv()

            zout[turn, c] = zin[turn, c] + term[pl.ds(at, piece), :]

            @pl.when(has_next)
            def _():
                z_copy(c).start()

            @pl.when(side == 0)
            def _():
                x_copy(c, zout).start()

            @pl.when(side == 1)
            def _():
                x_copy(c, zin).start()

            return 0

        lax.fori_loop(0, PIECES, chain, 0)

        def finish(c, _):
            at = pl.multiple_of(c * piece, piece)
            x_copy(c, zout).wait()
            before = zin[turn, c] + xin[turn, c]
            if turn == ITERS - 1:
                out_ref[pl.ds(at, piece), :] = before + term[pl.ds(at, piece), :]
            else:
                state[pl.ds(at, piece), :] = start_ref[pl.ds(at, piece), :] + before

            @pl.when(has_next)
            def _():
                z_copy(c).wait_send()

            return 0

        lax.fori_loop(0, PIECES, finish, 0)


def shards(
    n_tm,
    n_frame,
    start_state,
    initial_guess,
    noise_draws,
    timesteps,
    gain_space,
    gain_attention,
    time_weight,
    space_weight,
    attention_weight,
    output_weight,
):
    _, height, width, channels = start_state.shape
    cells = height * width
    share = cells // n_frame
    piece = cells // PIECES
    step_value = timesteps[0]
    time_value = step_value.astype(jnp.float32) / 1000.0
    coefficient = (0.5 + time_value) / math.sqrt(n_tm)
    scaling, offset = modulation(step_value, time_weight)
    rows = jnp.stack(
        [
            gain_space * scaling,
            offset,
            jnp.full((channels,), coefficient),
            jnp.full((channels,), time_value),
            gain_attention,
        ]
    )
    vmem = pl.BlockSpec(memory_space=pltpu.VMEM)
    f32, bf16 = jnp.float32, jnp.bfloat16
    dma = pltpu.SemaphoreType.DMA
    exchange = pltpu.VMEM((ITERS, n_frame, share, channels), bf16)
    sums = pltpu.VMEM((ITERS, PIECES, piece, channels), f32)
    total = pl.pallas_call(
        functools.partial(kernel, n_tm, n_frame, width),
        out_shape=jax.ShapeDtypeStruct((cells, channels), f32),
        in_specs=[vmem] * 7,
        out_specs=vmem,
        scratch_shapes=[
            pltpu.VMEM((cells, channels), f32),
            pltpu.VMEM((cells + 2 * width, 3 * channels), bf16),
            pltpu.VMEM((cells, channels), f32),
            pltpu.VMEM((cells, channels), f32),
            pltpu.VMEM((n_frame, share, 3 * channels), f32),
            exchange,
            exchange,
            exchange,
            exchange,
            sums,
            sums,
            sums,
            dma((ITERS, n_frame)),
            dma((ITERS, n_frame)),
            dma((ITERS, n_frame)),
            dma((ITERS, n_frame)),
            dma((ITERS, PIECES)),
            dma((ITERS, PIECES)),
            dma((ITERS, PIECES)),
            dma((ITERS, PIECES)),
        ],
        compiler_params=pltpu.CompilerParams(collective_id=0, has_side_effects=True),
    )(
        start_state.reshape(cells, channels),
        initial_guess.reshape(cells, channels),
        noise_draws.reshape(cells, channels),
        rows,
        space_weight,
        attention_weight,
        output_weight,
    )
    return start_state[None] + total.reshape(1, 1, height, width, channels)


def solution(mesh):
    return jax.shard_map(
        functools.partial(shards, mesh.shape["tm"], mesh.shape["frame"]),
        mesh=mesh,
        in_specs=(
            P("frame", None, None, None),
            P("tm", "frame", None, None, None),
            P("tm", "frame", None, None, None),
            P("tm"),
            P(),
            P(),
            P(),
            P(),
            P(),
            P(),
        ),
        out_specs=P("tm", "frame", None, None, None),
        check_vma=False,
    )
```

time: 243 us -> 68.3 us (0.28)
  waiting for transfers between devices: 149 us -> 0 us
  Pallas kernels: 0 us -> 63.1 us
  blocking collectives: 25.5 us -> 0 us
  other arithmetic: 19.7 us -> 1.97 us
  matrix products: 14.3 us -> 0.21 us
  between operations: 14.6 us -> 0.73 us
  local copies, waits for them, and re-layouts: 13.9 us -> 2.09 us
  starting transfers between devices: 3.49 us -> 0 us
    all_gather x2 -> x0, waiting for transfers between devices: 143 us -> none  [carried_in(): gathered = lax.all_gather(part, axis)]
    pallas_call x0 -> x1, Pallas kernels: none -> 63.1 us  [shards(): pl.pallas_call(functools.partial(kernel, n_tm, n_frame, width), out_shape...]
    all_to_all x3 -> x0, blocking collectives: 25.5 us -> none  [the longest x2 17.1 us: shards(): lax.all_to_all(normalize(mixed_state, gain_attention).astype(jnp.bfloat16...]
    add x13 -> x1, other arithmetic: 14.4 us -> 1.91 us  [shards(): return start_state[None] + total.reshape(1, 1, height, width, channels)]
    dot_general x8 -> x0, matrix products: 6.95 us -> none  [the longest x2 2.09 us: shards(): jnp.dot(evaluate_attended.reshape(-1, evaluate_attended.shape[-1]), outpu...]
    sub x2 -> x0, matrix products: 6.26 us -> none  [attend(): weights = jax.nn.softmax(scores, axis=-1).astype(jnp.bfloat16)]
    all_to_all x1 -> x0, waiting for transfers between devices: 5.91 us -> none  [shards(): lax.all_to_all(attended, 'frame', split_axis=0, concat_axis=1, tiled=True)]
    slice x3 -> x0, local copies, waits for them, and re-layouts: 5.54 us -> none  [the longest x2 5.22 us: attend(): projected[:, :, :, 2]]
  transfers between devices with their start and end apart: 3 -> 0, of which waited for: 3 -> 0; matrix products, arithmetic and copies ran while one was open for 0% -> 0% of each run, Pallas kernels for 0% -> 0%
where the time goes in v1:
time: 68.3 us; the launch traced here: 68.1 us
  Pallas kernels  63.1 us (92%)
  local copies, waits for them, and re-layouts  2.09 us (3%)
  other arithmetic  1.97 us (3%)
  between operations  0.73 us (1%)
    pallas_call x1, Pallas kernels, shards(): pl.pallas_call(functools.partial(kernel, n_tm, n_frame, width), out_shape...  63.1 us
    add x1, other arithmetic, shards(): return start_state[None] + total.reshape(1, 1, height, width, channels)  1.91 us
    unnamed x8, local copies, waits for them, and re-layouts  1.48 us

profile of v1, /device:TPU:24, one launch (start us, length us, event | category | flops | bytes accessed | tf_op | source)
XLA Modules:
  0.0 68.1 jit_solution(18075947948995101769)
XLA Ops:
  0.0 0.0 copy-start
  0.7 0.1 fusion.3
  0.8 0.1 copy-done
  0.9 0.2 fusion
  1.1 0.0 copy-start.2
  1.1 0.7 copy-done.2
  1.8 0.0 copy-start.3
  1.8 0.7 copy-done.3
  2.5 0.6 stack.15.rows_ref
  3.1 0.0 copy-start.1
  3.1 63.1 %shard_map.100 = f32[1024,128]{1,0:T(8,128)} custom-call(f32[1024,128]{1,0:T(8,128)} %bitcast.17, f32[1024,128]{1,0:T(8,128)} %bitcast.19, f32[1024,128]{1,0:T(8,128)} %bitcast.20, f32[5,128]{1,0:T(8,128)} %stack.15.rows_ref, bf16[1152,128]{1,0:T(8,128)(2,1)} %wconv_ref.1, bf16[128,384]{1,0:T(8,128)(2,1)} %wattn_ref.1, bf16[128,128]{1,0:T(8,128)(2,1)} %wout_ref.1), custom_call_target="tpu_custom_call" | custom-call | tf_op jit(solution)/shard_map/pallas_call | solution.py:339
  66.2 0.0 copy-done.1
  66.2 1.9 %bitcast_add_fusion = f32[1,1,32,32,128]{4,3,2,1,0:T(8,128)} fusion(f32[1,1,32,32,128]{4,3,2,1,0:T(8,128)} %bitcast.18, f32[1,32,32,128]{3,2,1,0:T(8,128)S(1)} %copy-done.1), kind=kLoop, calls=%fused_computation | loop fusion | flops 131072 | bytes 1572864 | tf_op jit(solution)/shard_map/add | solution.py:376
  (3 shorter events, 0.0 us)
Async XLA Ops:
  0.0 0.9 %copy-start = (f32[128,256]{1,0:T(8,128)S(1)}, f32[128,256]{1,0:T(8,128)}, u32[]{:S(2)}) copy-start(f32[128,256]{1,0:T(8,128)} %param.16) | copy-start | bytes 393220
  1.1 0.7 copy-start.2
  1.8 0.7 copy-start.3
  3.1 63.1 %copy-start.1 = (f32[1,32,32,128]{3,2,1,0:T(8,128)S(1)}, f32[1,32,32,128]{3,2,1,0:T(8,128)}, u32[]{:S(2)}) copy-start(f32[1,32,32,128]{3,2,1,0:T(8,128)} %param.10) | copy-start | bytes 1572868

commit v2 on v1

v2 whole, which is shorter than its diff:
```python
import functools
import math

import jax
import jax.numpy as jnp
from jax import lax
from jax.experimental import pallas as pl
from jax.experimental.pallas import tpu as pltpu
from jax.sharding import PartitionSpec as P

HEAD_DIM = 64
ITERS = 2
GROUPS = 2
X_TYPE = jnp.bfloat16
Z_TYPE = jnp.float32
EPS = 1e-06


def modulation(step_value, time_weight):
    channels = time_weight.shape[0]
    half_width = channels // 2
    frequency = jnp.exp(-math.log(10000.0) * jnp.arange(half_width, dtype=jnp.float32) / half_width)
    angles = step_value.astype(jnp.float32) * frequency
    encoded = jnp.concatenate([jnp.cos(angles), jnp.sin(angles)])[None, :]
    shifted = jnp.dot(
        encoded, time_weight, precision=lax.Precision.HIGHEST, preferred_element_type=jnp.float32
    )[0]
    return (1.0 + shifted[:channels], shifted[channels:])


def kernel(
    n_tm,
    n_frame,
    width,
    groups,
    start_ref,
    guess_ref,
    noise_ref,
    rows_ref,
    wconv_ref,
    wattn_ref,
    wout_ref,
    out_ref,
    state,
    taps,
    mixed,
    term,
    proj,
    ain,
    rin,
    aout,
    rout,
    pair_out,
    pair_in,
    zout,
    zin,
    back_out,
    back_in,
    in_send,
    in_recv,
    out_send,
    out_recv,
    pair_send,
    pair_recv,
    z_send,
    z_recv,
    back_send,
    back_recv,
):
    cells, channels = start_ref.shape
    share = cells // n_frame
    piece = share // groups
    half = piece // 2
    pieces = n_frame * groups
    me_tm = lax.axis_index("tm")
    me = lax.axis_index("frame")
    link = me_tm // 2
    side = lax.rem(me_tm, 2)
    links = n_tm // 2
    has_prev = link > 0
    has_next = link < links - 1

    def at_frame(f):
        return {"tm": me_tm, "frame": f}

    def at_tm(t):
        return {"tm": t, "frame": me}

    def peer(s):
        return lax.rem(me + s, n_frame)

    def sender(s):
        return lax.rem(me + n_frame - s, n_frame)

    barrier = pltpu.get_barrier_semaphore()

    def greet(device):
        pl.semaphore_signal(barrier, inc=1, device_id=device, device_id_type=pl.DeviceIdType.MESH)

    for s in range(1, n_frame):
        greet(at_frame(peer(s)))
    greet(at_tm(me_tm + 1 - 2 * side))

    @pl.when(has_prev)
    def _():
        greet(at_tm(me_tm - 2))

    @pl.when(has_next)
    def _():
        greet(at_tm(me_tm + 2))

    def meet():
        pl.semaphore_wait(barrier, n_frame + has_prev.astype(jnp.int32) + has_next.astype(jnp.int32))

    edge = jnp.zeros((width, 3 * channels), jnp.bfloat16)
    taps[0:width, :] = edge
    taps[cells + width : cells + 2 * width, :] = edge

    @pl.when(link == 0)
    def _():
        zin[...] = jnp.zeros_like(zin)

    gain_space = rows_ref[0:1, :]
    offset = rows_ref[1:2, :]
    coefficient = rows_ref[2:3, :]
    time_value = rows_ref[3:4, :]
    gain_attention = rows_ref[4:5, :]

    def inverse_rms(v):
        return lax.rsqrt(jnp.mean(v * v, axis=-1, keepdims=True) + EPS)

    column = lax.broadcasted_iota(jnp.int32, (piece, channels), 0) % width
    head_in = lax.broadcasted_iota(jnp.int32, (2 * channels, channels), 0) % channels // HEAD_DIM
    head_to = lax.broadcasted_iota(jnp.int32, (2 * channels, channels), 1) // HEAD_DIM
    gather_heads = jnp.where(head_in == head_to, 1.0, 0.0).astype(jnp.bfloat16)

    def make_taps(at, x):
        normed = x * inverse_rms(x) * gain_space + offset
        left = jnp.where(column == 0, 0.0, pltpu.roll(normed, 1, 0))
        right = jnp.where(column == width - 1, 0.0, pltpu.roll(normed, piece - 1, 0))
        to = pl.multiple_of(at + width, width)
        taps[pl.ds(to, piece), 0:channels] = left.astype(jnp.bfloat16)
        taps[pl.ds(to, piece), channels : 2 * channels] = normed.astype(jnp.bfloat16)
        taps[pl.ds(to, piece), 2 * channels : 3 * channels] = right.astype(jnp.bfloat16)

    def first_taps(i, _):
        at = pl.multiple_of(i * piece, piece)
        make_taps(at, guess_ref[pl.ds(at, piece), :])
        return 0

    def remote(src, dst, send, recv, device):
        return pltpu.make_async_remote_copy(
            src_ref=src,
            dst_ref=dst,
            send_sem=send,
            recv_sem=recv,
            device_id=device,
            device_id_type=pl.DeviceIdType.MESH,
        )

    for turn in range(ITERS):
        source = guess_ref if turn == 0 else state
        if turn == 0:
            lax.fori_loop(0, pieces, first_taps, 0)
            meet()

        def in_copy(s, g):
            return remote(
                ain.at[turn, g, peer(s)],
                rin.at[turn, g, me],
                in_send.at[turn, g, s],
                in_recv.at[turn, g, s],
                at_frame(peer(s)),
            )

        def out_copy(s, g):
            return remote(
                aout.at[turn, g, peer(s)],
                rout.at[turn, g, me],
                out_send.at[turn, g, s],
                out_recv.at[turn, g, s],
                at_frame(peer(s)),
            )

        def pair_copy(i):
            return remote(
                pair_out.at[turn, i],
                pair_in.at[turn, i],
                pair_send.at[turn, i],
                pair_recv.at[turn, i],
                at_tm(me_tm + 1 - 2 * side),
            )

        def z_copy(i):
            return remote(
                zout.at[turn, i], zin.at[turn, i], z_send.at[turn, i], z_recv.at[turn, i], at_tm(me_tm + 2)
            )

        def back_copy(i):
            return remote(
                back_out.at[turn, i],
                back_in.at[turn, i],
                back_send.at[turn, i],
                back_recv.at[turn, i],
                at_tm(me_tm + 1 - 2 * side),
            )

        def mix(q, g):
            at = pl.multiple_of(q * share + g * piece, piece)
            total = jnp.zeros((piece, channels), jnp.float32)
            for row in range(3):
                start = pl.multiple_of(at + row * width, width)
                total += jnp.dot(
                    taps[pl.ds(start, piece), :],
                    wconv_ref[row * 3 * channels : (row + 1) * 3 * channels, :],
                    preferred_element_type=jnp.float32,
                )
            value = source[pl.ds(at, piece), :] + total / (1.0 + jnp.exp(-total))
            mixed[pl.ds(at, piece), :] = value
            return (value * inverse_rms(value) * gain_attention).astype(jnp.bfloat16)

        def project(f, g):
            proj[g, f] = (
                jnp.dot(rin[turn, g, f], wattn_ref[...], preferred_element_type=jnp.float32)
                .astype(jnp.bfloat16)
                .astype(jnp.float32)
            )

        def attend(f, g):
            query = proj[g, f, :, 0:channels]
            products = (query[None] * proj[g, :, :, channels : 2 * channels]).reshape(-1, channels)
            high = products.astype(jnp.bfloat16)
            low = (products - high.astype(jnp.float32)).astype(jnp.bfloat16)
            scores = jnp.dot(
                jnp.concatenate([high, low], axis=-1), gather_heads, preferred_element_type=jnp.float32
            ).reshape(n_frame, piece, channels) * (1.0 / math.sqrt(HEAD_DIM))
            raised = jnp.exp(scores - jnp.max(scores, axis=0, keepdims=True))
            weights = raised / jnp.sum(raised, axis=0, keepdims=True)
            weights = weights.astype(jnp.bfloat16).astype(jnp.float32)
            return jnp.sum(weights * proj[g, :, :, 2 * channels : 3 * channels], axis=0).astype(jnp.bfloat16)

        def place(i):
            return pl.multiple_of(sender(i % n_frame) * share + i // n_frame * piece, piece)

        for g in range(groups):

            def mix_and_send(s, _):
                q = peer(s)
                ain[turn, g, q] = mix(q, g)
                in_copy(s, g).start()
                return 0

            lax.fori_loop(1, n_frame, mix_and_send, 0)
            rin[turn, g, me] = mix(me, g)
            project(me, g)

        for g in range(groups):

            def arrive(s, _):
                in_copy(s, g).wait_recv()
                project(sender(s), g)
                return 0

            lax.fori_loop(1, n_frame, arrive, 0)

            def attend_and_send(s, _):
                f = peer(s)
                aout[turn, g, f] = attend(f, g)
                out_copy(s, g).start()
                return 0

            lax.fori_loop(1, n_frame, attend_and_send, 0)
            rout[turn, g, me] = attend(me, g)

        for g in range(groups):

            def close(s):
                q = sender(s)
                i = g * n_frame + s
                at = pl.multiple_of(q * share + g * piece, piece)
                drift = mixed[pl.ds(at, piece), :] + jnp.dot(
                    rout[turn, g, q], wout_ref[...], preferred_element_type=jnp.float32
                )
                term[pl.ds(at, piece), :] = coefficient * (drift + time_value * noise_ref[pl.ds(at, piece), :])
                other = pl.multiple_of(at + (1 - side) * half, half)
                pair_out[turn, i] = term[pl.ds(other, half), :].astype(pair_out.dtype)
                pair_copy(i).start()

            close(0)

            def land(s, _):
                out_copy(s, g).wait_recv()
                close(s)
                return 0

            lax.fori_loop(1, n_frame, land, 0)

        def chain(i, _):
            own = pl.multiple_of(place(i) + side * half, half)
            mine = term[pl.ds(own, half), :]
            pair_copy(i).wait_recv()
            both = mine + pair_in[turn, i].astype(jnp.float32)

            @pl.when(has_prev)
            def _():
                z_copy(i).wait_recv()

            earlier = zin[turn, i].astype(jnp.float32)

            @pl.when(has_next)
            def _():
                zout[turn, i] = (earlier + both).astype(zout.dtype)
                z_copy(i).start()

            back_out[turn, i] = jnp.where(side == 0, earlier + mine, earlier).astype(back_out.dtype)
            back_copy(i).start()
            return 0

        lax.fori_loop(0, pieces, chain, 0)

        def finish(i, _):
            at = place(i)
            own = pl.multiple_of(at + side * half, half)
            other = pl.multiple_of(at + (1 - side) * half, half)
            last = turn == ITERS - 1
            base, target = (term, out_ref) if last else (start_ref, state)
            earlier = zin[turn, i].astype(jnp.float32)
            first = jnp.where(side == 0, earlier, earlier + pair_in[turn, i].astype(jnp.float32))
            target[pl.ds(own, half), :] = base[pl.ds(own, half), :] + first
            back_copy(i).wait_recv()
            target[pl.ds(other, half), :] = base[pl.ds(other, half), :] + back_in[turn, i].astype(jnp.float32)
            if not last:
                make_taps(at, state[pl.ds(at, piece), :])
            return 0

        lax.fori_loop(0, pieces, finish, 0)

        def sent(i, _):
            pair_copy(i).wait_send()
            back_copy(i).wait_send()

            @pl.when(has_next)
            def _():
                z_copy(i).wait_send()

            return 0

        lax.fori_loop(0, pieces, sent, 0)

        for g in range(groups):

            def left(s, _):
                in_copy(s, g).wait_send()
                out_copy(s, g).wait_send()
                return 0

            lax.fori_loop(1, n_frame, left, 0)


def shards(
    n_tm,
    n_frame,
    start_state,
    initial_guess,
    noise_draws,
    timesteps,
    gain_space,
    gain_attention,
    time_weight,
    space_weight,
    attention_weight,
    output_weight,
):
    _, height, width, channels = start_state.shape
    cells = height * width
    share = cells // n_frame
    groups = GROUPS if share // width % GROUPS == 0 else 1
    piece = share // groups
    pieces = n_frame * groups
    step_value = timesteps[0]
    time_value = step_value.astype(jnp.float32) / 1000.0
    coefficient = (0.5 + time_value) / math.sqrt(n_tm)
    scaling, offset = modulation(step_value, time_weight)
    rows = jnp.stack(
        [
            gain_space * scaling,
            offset,
            jnp.full((channels,), coefficient),
            jnp.full((channels,), time_value),
            gain_attention,
        ]
    )
    vmem = pl.BlockSpec(memory_space=pltpu.VMEM)
    f32, bf16 = jnp.float32, jnp.bfloat16
    dma = pltpu.SemaphoreType.DMA
    exchange = pltpu.VMEM((ITERS, groups, n_frame, piece, channels), bf16)
    cross = pltpu.VMEM((ITERS, pieces, piece // 2, channels), X_TYPE)
    along = pltpu.VMEM((ITERS, pieces, piece // 2, channels), Z_TYPE)
    total = pl.pallas_call(
        functools.partial(kernel, n_tm, n_frame, width, groups),
        out_shape=jax.ShapeDtypeStruct((cells, channels), f32),
        in_specs=[vmem] * 7,
        out_specs=vmem,
        scratch_shapes=[
            pltpu.VMEM((cells, channels), f32),
            pltpu.VMEM((cells + 2 * width, 3 * channels), bf16),
            pltpu.VMEM((cells, channels), f32),
            pltpu.VMEM((cells, channels), f32),
            pltpu.VMEM((groups, n_frame, piece, 3 * channels), f32),
            exchange,
            exchange,
            exchange,
            exchange,
            cross,
            cross,
            along,
            along,
            cross,
            cross,
            *([dma((ITERS, groups, n_frame))] * 4),
            *([dma((ITERS, pieces))] * 6),
        ],
        compiler_params=pltpu.CompilerParams(collective_id=0, has_side_effects=True),
    )(
        start_state.reshape(cells, channels),
        initial_guess.reshape(cells, channels),
        noise_draws.reshape(cells, channels),
        rows,
        space_weight,
        attention_weight,
        output_weight,
    )
    return start_state[None] + total.reshape(1, 1, height, width, channels)


def solution(mesh):
    return jax.shard_map(
        functools.partial(shards, mesh.shape["tm"], mesh.shape["frame"]),
        mesh=mesh,
        in_specs=(
            P("frame", None, None, None),
            P("tm", "frame", None, None, None),
            P("tm", "frame", None, None, None),
            P("tm"),
            P(),
            P(),
            P(),
            P(),
            P(),
            P(),
        ),
        out_specs=P("tm", "frame", None, None, None),
        check_vma=False,
    )
```

time: 68.3 us -> 53.1 us (0.78)
  Pallas kernels: 63.1 us -> 47.8 us
    pallas_call x1, Pallas kernels: 63.1 us -> 47.8 us  [shards(): pl.pallas_call(functools.partial(kernel, n_tm, n_frame, width, groups), o...]
where the time goes in v2:
time: 53.1 us; the launch traced here: 52.8 us
  Pallas kernels  47.8 us (90%)
  local copies, waits for them, and re-layouts  2.09 us (4%)
  other arithmetic  1.97 us (4%)
  between operations  0.73 us (1%)
    pallas_call x1, Pallas kernels, shards(): pl.pallas_call(functools.partial(kernel, n_tm, n_frame, width, groups), o...  47.8 us
    add x1, other arithmetic, shards(): return start_state[None] + total.reshape(1, 1, height, width, channels)  1.91 us
    unnamed x8, local copies, waits for them, and re-layouts  1.48 us

profile of v2, /device:TPU:24, one launch (start us, length us, event | category | flops | bytes accessed | tf_op | source)
XLA Modules:
  0.0 52.8 jit_solution(14317805571648461547)
XLA Ops:
  0.0 0.0 copy-start
  0.7 0.1 fusion.3
  0.8 0.1 copy-done
  0.9 0.2 fusion
  1.1 0.0 copy-start.2
  1.1 0.7 %copy-done.2 = f32[128]{0:T(128)S(1)} copy-done((f32[128]{0:T(128)S(1)}, f32[128]{0:T(128)}, u32[]{:S(2)}) %copy-start.2) | copy-done | bytes 536
  1.8 0.0 copy-start.3
  1.8 0.7 %copy-done.3 = f32[128]{0:T(128)S(1)} copy-done((f32[128]{0:T(128)S(1)}, f32[128]{0:T(128)}, u32[]{:S(2)}) %copy-start.3) | copy-done | bytes 536
  2.5 0.6 %stack.15.rows_ref = f32[5,128]{1,0:T(8,128)} concatenate(f32[1,128]{1,0:T(1,128)S(1)} %get-tuple-element.6, f32[1,128]{1,0:T(1,128)S(1)} %get-tuple-element.5, f32[1,128]{1,0:T(1,128)S(1)} %stack_broadcast_in_dim.6, f32[1,128]{1,0:T(1,128)S(1)} %stack_broadcast_in_dim.7, f32[1,128]{1,0:T(1,128)S(1)} %bitcast.22), dimensions={0} | concatenate | bytes 5120 | tf_op jit(solution)/shard_map/stack | solution.py:384
  3.1 0.0 copy-start.1
  3.1 47.8 %shard_map.100 = f32[1024,128]{1,0:T(8,128)} custom-call(f32[1024,128]{1,0:T(8,128)} %bitcast.17, f32[1024,128]{1,0:T(8,128)} %bitcast.19, f32[1024,128]{1,0:T(8,128)} %bitcast.20, f32[5,128]{1,0:T(8,128)} %stack.15.rows_ref, bf16[1152,128]{1,0:T(8,128)(2,1)} %wconv_ref.1, bf16[128,384]{1,0:T(8,128)(2,1)} %wattn_ref.1, bf16[128,128]{1,0:T(8,128)(2,1)} %wout_ref.1), custom_call_target="tpu_custom_call" | custom-call | tf_op jit(solution)/shard_map/pallas_call | solution.py:399
  50.9 0.0 copy-done.1
  50.9 1.9 %bitcast_add_fusion = f32[1,1,32,32,128]{4,3,2,1,0:T(8,128)} fusion(f32[1,1,32,32,128]{4,3,2,1,0:T(8,128)} %bitcast.18, f32[1,32,32,128]{3,2,1,0:T(8,128)S(1)} %copy-done.1), kind=kLoop, calls=%fused_computation | loop fusion | flops 131072 | bytes 1572864 | tf_op jit(solution)/shard_map/add | solution.py:433
  (3 shorter events, 0.0 us)
Async XLA Ops:
  0.0 0.9 %copy-start = (f32[128,256]{1,0:T(8,128)S(1)}, f32[128,256]{1,0:T(8,128)}, u32[]{:S(2)}) copy-start(f32[128,256]{1,0:T(8,128)} %param.16) | copy-start | bytes 393220
  1.1 0.7 %copy-start.2 = (f32[128]{0:T(128)S(1)}, f32[128]{0:T(128)}, u32[]{:S(2)}) copy-start(f32[128]{0:T(128)} %param.14) | copy-start | bytes 1540
  1.8 0.7 %copy-start.3 = (f32[128]{0:T(128)S(1)}, f32[128]{0:T(128)}, u32[]{:S(2)}) copy-start(f32[128]{0:T(128)} %param.15) | copy-start | bytes 1540
  3.1 47.8 %copy-start.1 = (f32[1,32,32,128]{3,2,1,0:T(8,128)S(1)}, f32[1,32,32,128]{3,2,1,0:T(8,128)}, u32[]{:S(2)}) copy-start(f32[1,32,32,128]{3,2,1,0:T(8,128)} %param.10) | copy-start | bytes 1572868

commit v3 on v2

--- a/solution.py
+++ b/solution.py
@@ -12,7 +12,7 @@
 ITERS = 2
 GROUPS = 2
 X_TYPE = jnp.bfloat16
-Z_TYPE = jnp.float32
+Z_TYPES = (jnp.bfloat16, jnp.float32)
 EPS = 1e-06
 
 
@@ -52,8 +52,10 @@
     rout,
     pair_out,
     pair_in,
-    zout,
-    zin,
+    zout_first,
+    zout_last,
+    zin_first,
+    zin_last,
     back_out,
     back_in,
     in_send,
@@ -118,7 +120,8 @@
 
     @pl.when(link == 0)
     def _():
-        zin[...] = jnp.zeros_like(zin)
+        zin_first[...] = jnp.zeros_like(zin_first)
+        zin_last[...] = jnp.zeros_like(zin_last)
 
     gain_space = rows_ref[0:1, :]
     offset = rows_ref[1:2, :]
@@ -160,6 +163,7 @@
 
     for turn in range(ITERS):
         source = guess_ref if turn == 0 else state
+        zout, zin = (zout_last, zin_last) if turn == ITERS - 1 else (zout_first, zin_first)
         if turn == 0:
             lax.fori_loop(0, pieces, first_taps, 0)
             meet()
@@ -395,7 +399,7 @@
     dma = pltpu.SemaphoreType.DMA
     exchange = pltpu.VMEM((ITERS, groups, n_frame, piece, channels), bf16)
     cross = pltpu.VMEM((ITERS, pieces, piece // 2, channels), X_TYPE)
-    along = pltpu.VMEM((ITERS, pieces, piece // 2, channels), Z_TYPE)
+    along = [pltpu.VMEM((ITERS, pieces, piece // 2, channels), kind) for kind in Z_TYPES]
     total = pl.pallas_call(
         functools.partial(kernel, n_tm, n_frame, width, groups),
         out_shape=jax.ShapeDtypeStruct((cells, channels), f32),
@@ -413,8 +417,8 @@
             exchange,
             cross,
             cross,
-            along,
-            along,
+            *along,
+            *along,
             cross,
             cross,
             *([dma((ITERS, groups, n_frame))] * 4),

time: 53.1 us -> 51.4 us (0.968)
  Pallas kernels: 47.8 us -> 46.1 us
    pallas_call x1, Pallas kernels: 47.8 us -> 46.1 us  [shards(): pl.pallas_call(functools.partial(kernel, n_tm, n_frame, width, groups), o...]
where the time goes in v3:
time: 51.4 us; the launch traced here: 51.2 us
  Pallas kernels  46.1 us (90%)
  local copies, waits for them, and re-layouts  2.09 us (4%)
  other arithmetic  1.97 us (4%)
  between operations  0.73 us (1%)
    pallas_call x1, Pallas kernels, shards(): pl.pallas_call(functools.partial(kernel, n_tm, n_frame, width, groups), o...  46.1 us
    add x1, other arithmetic, shards(): return start_state[None] + total.reshape(1, 1, height, width, channels)  1.91 us
    unnamed x8, local copies, waits for them, and re-layouts  1.48 us

profile of v3, /device:TPU:24, one launch (start us, length us, event | category | flops | bytes accessed | tf_op | source)
XLA Modules:
  0.0 51.2 jit_solution(3208913461174766911)
XLA Ops:
  0.0 0.0 copy-start
  0.7 0.1 fusion.3
  0.8 0.1 copy-done
  0.9 0.2 fusion
  1.1 0.0 copy-start.2
  1.1 0.7 %copy-done.2 = f32[128]{0:T(128)S(1)} copy-done((f32[128]{0:T(128)S(1)}, f32[128]{0:T(128)}, u32[]{:S(2)}) %copy-start.2) | copy-done | bytes 536
  1.8 0.0 copy-start.3
  1.8 0.7 %copy-done.3 = f32[128]{0:T(128)S(1)} copy-done((f32[128]{0:T(128)S(1)}, f32[128]{0:T(128)}, u32[]{:S(2)}) %copy-start.3) | copy-done | bytes 536
  2.5 0.6 %stack.15.rows_ref = f32[5,128]{1,0:T(8,128)} concatenate(f32[1,128]{1,0:T(1,128)S(1)} %get-tuple-element.6, f32[1,128]{1,0:T(1,128)S(1)} %get-tuple-element.5, f32[1,128]{1,0:T(1,128)S(1)} %stack_broadcast_in_dim.6, f32[1,128]{1,0:T(1,128)S(1)} %stack_broadcast_in_dim.7, f32[1,128]{1,0:T(1,128)S(1)} %bitcast.22), dimensions={0} | concatenate | bytes 5120 | tf_op jit(solution)/shard_map/stack | solution.py:388
  3.1 0.0 copy-start.1
  3.1 46.1 %shard_map.100 = f32[1024,128]{1,0:T(8,128)} custom-call(f32[1024,128]{1,0:T(8,128)} %bitcast.17, f32[1024,128]{1,0:T(8,128)} %bitcast.19, f32[1024,128]{1,0:T(8,128)} %bitcast.20, f32[5,128]{1,0:T(8,128)} %stack.15.rows_ref, bf16[1152,128]{1,0:T(8,128)(2,1)} %wconv_ref.1, bf16[128,384]{1,0:T(8,128)(2,1)} %wattn_ref.1, bf16[128,128]{1,0:T(8,128)(2,1)} %wout_ref.1), custom_call_target="tpu_custom_call" | custom-call | tf_op jit(solution)/shard_map/pallas_call | solution.py:403
  49.2 0.0 copy-done.1
  49.2 1.9 %bitcast_add_fusion = f32[1,1,32,32,128]{4,3,2,1,0:T(8,128)} fusion(f32[1,1,32,32,128]{4,3,2,1,0:T(8,128)} %bitcast.18, f32[1,32,32,128]{3,2,1,0:T(8,128)S(1)} %copy-done.1), kind=kLoop, calls=%fused_computation | loop fusion | flops 131072 | bytes 1572864 | tf_op jit(solution)/shard_map/add | solution.py:437
  (3 shorter events, 0.0 us)
Async XLA Ops:
  0.0 0.9 %copy-start = (f32[128,256]{1,0:T(8,128)S(1)}, f32[128,256]{1,0:T(8,128)}, u32[]{:S(2)}) copy-start(f32[128,256]{1,0:T(8,128)} %param.16) | copy-start | bytes 393220
  1.1 0.7 %copy-start.2 = (f32[128]{0:T(128)S(1)}, f32[128]{0:T(128)}, u32[]{:S(2)}) copy-start(f32[128]{0:T(128)} %param.14) | copy-start | bytes 1540
  1.8 0.7 %copy-start.3 = (f32[128]{0:T(128)S(1)}, f32[128]{0:T(128)}, u32[]{:S(2)}) copy-start(f32[128]{0:T(128)} %param.15) | copy-start | bytes 1540
  3.1 46.2 %copy-start.1 = (f32[1,32,32,128]{3,2,1,0:T(8,128)S(1)}, f32[1,32,32,128]{3,2,1,0:T(8,128)}, u32[]{:S(2)}) copy-start(f32[1,32,32,128]{3,2,1,0:T(8,128)} %param.10) | copy-start | bytes 1572868

commit v4 on v3

--- a/solution.py
+++ b/solution.py
@@ -209,26 +209,34 @@
                 at_tm(me_tm + 1 - 2 * side),
             )
 
-        def mix(q, g):
-            at = pl.multiple_of(q * share + g * piece, piece)
-            total = jnp.zeros((piece, channels), jnp.float32)
+        def rows_of(q, g):
+            return pl.multiple_of(q * share + g * piece, piece)
+
+        def mix(g):
+            everyone = range(n_frame)
+            total = jnp.zeros((n_frame * piece, channels), jnp.float32)
             for row in range(3):
-                start = pl.multiple_of(at + row * width, width)
+                near = [taps[pl.ds(rows_of(q, g) + row * width, piece), :] for q in everyone]
                 total += jnp.dot(
-                    taps[pl.ds(start, piece), :],
+                    jnp.concatenate(near, axis=0),
                     wconv_ref[row * 3 * channels : (row + 1) * 3 * channels, :],
                     preferred_element_type=jnp.float32,
                 )
-            value = source[pl.ds(at, piece), :] + total / (1.0 + jnp.exp(-total))
-            mixed[pl.ds(at, piece), :] = value
-            return (value * inverse_rms(value) * gain_attention).astype(jnp.bfloat16)
-
-        def project(f, g):
-            proj[g, f] = (
-                jnp.dot(rin[turn, g, f], wattn_ref[...], preferred_element_type=jnp.float32)
+            here = jnp.concatenate([source[pl.ds(rows_of(q, g), piece), :] for q in everyone], axis=0)
+            value = here + total / (1.0 + jnp.exp(-total))
+            normed = (value * inverse_rms(value) * gain_attention).astype(jnp.bfloat16)
+            for q in everyone:
+                mixed[pl.ds(rows_of(q, g), piece), :] = value[q * piece : (q + 1) * piece]
+                ain[turn, g, q] = normed[q * piece : (q + 1) * piece]
+
+        def project(g, blocks, owners):
+            result = (
+                jnp.dot(jnp.concatenate(blocks, axis=0), wattn_ref[...], preferred_element_type=jnp.float32)
                 .astype(jnp.bfloat16)
                 .astype(jnp.float32)
             )
+            for at, f in enumerate(owners):
+                proj[g, f] = result[at * piece : (at + 1) * piece]
 
         def attend(f, g):
             query = proj[g, f, :, 0:channels]
@@ -239,65 +247,59 @@
                 jnp.concatenate([high, low], axis=-1), gather_heads, preferred_element_type=jnp.float32
             ).reshape(n_frame, piece, channels) * (1.0 / math.sqrt(HEAD_DIM))
             raised = jnp.exp(scores - jnp.max(scores, axis=0, keepdims=True))
-            weights = raised / jnp.sum(raised, axis=0, keepdims=True)
+            weights = raised * (1.0 / jnp.sum(raised, axis=0, keepdims=True))
             weights = weights.astype(jnp.bfloat16).astype(jnp.float32)
-            return jnp.sum(weights * proj[g, :, :, 2 * channels : 3 * channels], axis=0).astype(jnp.bfloat16)
+            aout[turn, g, f] = jnp.sum(weights * proj[g, :, :, 2 * channels : 3 * channels], axis=0).astype(
+                jnp.bfloat16
+            )
+
+        def close(g, blocks, owners):
+            result = jnp.dot(
+                jnp.concatenate(blocks, axis=0), wout_ref[...], preferred_element_type=jnp.float32
+            )
+            for at, q in enumerate(owners):
+                rows = pl.ds(rows_of(q, g), piece)
+                drift = mixed[rows, :] + result[at * piece : (at + 1) * piece]
+                term[rows, :] = coefficient * (drift + time_value * noise_ref[rows, :])
+
+        def share_pairs(g, steps):
+            for s in steps:
+                other = pl.multiple_of(rows_of(sender(s), g) + (1 - side) * half, half)
+                pair_out[turn, g * n_frame + s] = term[pl.ds(other, half), :].astype(pair_out.dtype)
+            for s in steps:
+                pair_copy(g * n_frame + s).start()
 
         def place(i):
             return pl.multiple_of(sender(i % n_frame) * share + i // n_frame * piece, piece)
 
+        others = range(1, n_frame)
         for g in range(groups):
-
-            def mix_and_send(s, _):
-                q = peer(s)
-                ain[turn, g, q] = mix(q, g)
+            mix(g)
+            for s in others:
                 in_copy(s, g).start()
-                return 0
-
-            lax.fori_loop(1, n_frame, mix_and_send, 0)
-            rin[turn, g, me] = mix(me, g)
-            project(me, g)
-
         for g in range(groups):
-
-            def arrive(s, _):
+            project(g, [ain[turn, g, me]], [me])
+
+        for g in range(groups):
+            for s in others:
                 in_copy(s, g).wait_recv()
-                project(sender(s), g)
-                return 0
-
-            lax.fori_loop(1, n_frame, arrive, 0)
+            project(g, [rin[turn, g, sender(s)] for s in others], [sender(s) for s in others])
 
             def attend_and_send(s, _):
-                f = peer(s)
-                aout[turn, g, f] = attend(f, g)
+                attend(peer(s), g)
                 out_copy(s, g).start()
                 return 0
 
             lax.fori_loop(1, n_frame, attend_and_send, 0)
-            rout[turn, g, me] = attend(me, g)
+            attend(me, g)
 
         for g in range(groups):
-
-            def close(s):
-                q = sender(s)
-                i = g * n_frame + s
-                at = pl.multiple_of(q * share + g * piece, piece)
-                drift = mixed[pl.ds(at, piece), :] + jnp.dot(
-                    rout[turn, g, q], wout_ref[...], preferred_element_type=jnp.float32
-                )
-                term[pl.ds(at, piece), :] = coefficient * (drift + time_value * noise_ref[pl.ds(at, piece), :])
-                other = pl.multiple_of(at + (1 - side) * half, half)
-                pair_out[turn, i] = term[pl.ds(other, half), :].astype(pair_out.dtype)
-                pair_copy(i).start()
-
-            close(0)
-
-            def land(s, _):
+            close(g, [aout[turn, g, me]], [me])
+            share_pairs(g, [0])
+            for s in others:
                 out_copy(s, g).wait_recv()
-                close(s)
-                return 0
-
-            lax.fori_loop(1, n_frame, land, 0)
+            close(g, [rout[turn, g, sender(s)] for s in others], [sender(s) for s in others])
+            share_pairs(g, others)
 
         def chain(i, _):
             own = pl.multiple_of(place(i) + side * half, half)
@@ -319,8 +321,6 @@
             back_out[turn, i] = jnp.where(side == 0, earlier + mine, earlier).astype(back_out.dtype)
             back_copy(i).start()
             return 0
-
-        lax.fori_loop(0, pieces, chain, 0)
 
         def finish(i, _):
             at = place(i)
@@ -337,6 +337,12 @@
                 make_taps(at, state[pl.ds(at, piece), :])
             return 0
 
+        def chain_and_finish(i, _):
+            chain(i, 0)
+            finish(i - LAG, 0)
+            return 0
+
+        lax.fori_loop(0, pieces, chain, 0)
         lax.fori_loop(0, pieces, finish, 0)
 
         def sent(i, _):

time: 51.4 us -> 51.1 us (level)
  no operation moved by 1% of the time
where the time goes in v4:
time: 51.1 us; the launch traced here: 50.9 us
  Pallas kernels  45.9 us (90%)
  local copies, waits for them, and re-layouts  2.09 us (4%)
  other arithmetic  1.97 us (4%)
  between operations  0.73 us (1%)
    pallas_call x1, Pallas kernels, shards(): pl.pallas_call(functools.partial(kernel, n_tm, n_frame, width, groups), o...  45.9 us
    add x1, other arithmetic, shards(): return start_state[None] + total.reshape(1, 1, height, width, channels)  1.91 us
    unnamed x8, local copies, waits for them, and re-layouts  1.48 us

profile of v4, /device:TPU:24, one launch (start us, length us, event | category | flops | bytes accessed | tf_op | source)
XLA Modules:
  0.0 50.9 jit_solution(16873317468384125585)
XLA Ops:
  0.0 0.0 copy-start
  0.7 0.1 fusion.3
  0.8 0.1 copy-done
  0.9 0.2 fusion
  1.1 0.0 copy-start.2
  1.1 0.7 %copy-done.2 = f32[128]{0:T(128)S(1)} copy-done((f32[128]{0:T(128)S(1)}, f32[128]{0:T(128)}, u32[]{:S(2)}) %copy-start.2) | copy-done | bytes 536
  1.8 0.0 copy-start.3
  1.8 0.7 %copy-done.3 = f32[128]{0:T(128)S(1)} copy-done((f32[128]{0:T(128)S(1)}, f32[128]{0:T(128)}, u32[]{:S(2)}) %copy-start.3) | copy-done | bytes 536
  2.5 0.6 %stack.15.rows_ref = f32[5,128]{1,0:T(8,128)} concatenate(f32[1,128]{1,0:T(1,128)S(1)} %get-tuple-element.6, f32[1,128]{1,0:T(1,128)S(1)} %get-tuple-element.5, f32[1,128]{1,0:T(1,128)S(1)} %stack_broadcast_in_dim.6, f32[1,128]{1,0:T(1,128)S(1)} %stack_broadcast_in_dim.7, f32[1,128]{1,0:T(1,128)S(1)} %bitcast.22), dimensions={0} | concatenate | bytes 5120 | tf_op jit(solution)/shard_map/stack | solution.py:394
  3.1 0.0 copy-start.1
  3.1 45.9 %shard_map.100 = f32[1024,128]{1,0:T(8,128)} custom-call(f32[1024,128]{1,0:T(8,128)} %bitcast.17, f32[1024,128]{1,0:T(8,128)} %bitcast.19, f32[1024,128]{1,0:T(8,128)} %bitcast.20, f32[5,128]{1,0:T(8,128)} %stack.15.rows_ref, bf16[1152,128]{1,0:T(8,128)(2,1)} %wconv_ref.1, bf16[128,384]{1,0:T(8,128)(2,1)} %wattn_ref.1, bf16[128,128]{1,0:T(8,128)(2,1)} %wout_ref.1), custom_call_target="tpu_custom_call" | custom-call | tf_op jit(solution)/shard_map/pallas_call | solution.py:409
  49.0 0.0 copy-done.1
  49.0 1.9 %bitcast_add_fusion = f32[1,1,32,32,128]{4,3,2,1,0:T(8,128)} fusion(f32[1,1,32,32,128]{4,3,2,1,0:T(8,128)} %bitcast.18, f32[1,32,32,128]{3,2,1,0:T(8,128)S(1)} %copy-done.1), kind=kLoop, calls=%fused_computation | loop fusion | flops 131072 | bytes 1572864 | tf_op jit(solution)/shard_map/add | solution.py:443
  (3 shorter events, 0.0 us)
Async XLA Ops:
  0.0 0.9 %copy-start = (f32[128,256]{1,0:T(8,128)S(1)}, f32[128,256]{1,0:T(8,128)}, u32[]{:S(2)}) copy-start(f32[128,256]{1,0:T(8,128)} %param.16) | copy-start | bytes 393220
  1.1 0.7 %copy-start.2 = (f32[128]{0:T(128)S(1)}, f32[128]{0:T(128)}, u32[]{:S(2)}) copy-start(f32[128]{0:T(128)} %param.14) | copy-start | bytes 1540
  1.8 0.7 %copy-start.3 = (f32[128]{0:T(128)S(1)}, f32[128]{0:T(128)}, u32[]{:S(2)}) copy-start(f32[128]{0:T(128)} %param.15) | copy-start | bytes 1540
  3.1 45.9 %copy-start.1 = (f32[1,32,32,128]{3,2,1,0:T(8,128)S(1)}, f32[1,32,32,128]{3,2,1,0:T(8,128)}, u32[]{:S(2)}) copy-start(f32[1,32,32,128]{3,2,1,0:T(8,128)} %param.10) | copy-start | bytes 1572868
